TPU v7x, 256 devices: a whole 4x4x8 slice. The times are simulated.
256 devices in a mesh: gx: 4 (over y), gy: 8 (over x, core), gz: 8 (over z).
Axes of the slice: x: 4, y: 4, z: 8, core: 2. Of those that a mesh axis runs over, the one named last changes fastest.
Arguments:
- source: float32 [64, 128, 1024], P('gx', 'gy', 'gz'), may hold values from -5 to 5
- conductance: float32 [64, 128, 1024], P('gx', 'gy', 'gz'), may hold values from 0.2 to 2
- pressure_start: float32 [64, 128, 1024], P('gx', 'gy', 'gz'), may hold values from -6 to 6
Outputs:
- pressure: float32 [64, 128, 1024], P('gx', 'gy', 'gz')
- residual: float32 [64, 128, 1024], P('gx', 'gy', 'gz')
All inputs are finite; a program needn't handle non-finite values.
Results may differ from a plain program's by a relative error of at most 0.0003.
Values sent between devices are 32-bit elements; how exact they have to be, the bound alone decides.
A program may use at most 384 MiB of HBM per device.

v0:
```python
import jax
import jax.numpy as jnp
from jax import lax
from jax.sharding import PartitionSpec as P

LEVELS = 3
DEG = 3
COARSE_ITERS = 12
SHIFT = 0.001
UPPER_BOUND = 2.0
SMOOTH_FLOOR = 0.5
COARSE_FLOOR = 0.05


def extended(cells, sides, width):
    for axis, dim in sides:
        count = lax.axis_size(axis)
        head = lax.slice_in_dim(cells, 0, width, axis=dim)
        tail = lax.slice_in_dim(cells, cells.shape[dim] - width, cells.shape[dim], axis=dim)
        cells = jnp.concatenate(
            [
                lax.ppermute(tail, axis, [(i, (i + 1) % count) for i in range(count)]),
                cells,
                lax.ppermute(head, axis, [((i + 1) % count, i) for i in range(count)]),
            ],
            axis=dim,
        )
    return cells


def chebyshev_weights(number, floor_value):
    centre = 0.5 * (UPPER_BOUND + floor_value)
    half_width = 0.5 * (UPPER_BOUND - floor_value)
    ratio = centre / half_width
    factor = 1.0 / ratio
    weights = [(0.0, 1.0 / centre)]
    for _ in range(1, number):
        factor_next = 1.0 / (2.0 * ratio - factor)
        weights.append((factor_next * factor, 2.0 * factor_next / half_width))
        factor = factor_next
    return weights


def operate_global(field, conduct):
    total = SHIFT * field
    for axis_id in range(3):
        for offset in (1, -1):
            face = 0.5 * (conduct + jnp.roll(conduct, -offset, axis_id))
            total = total + face * (field - jnp.roll(field, -offset, axis_id))
    return total


def diagonal_global(conduct):
    total = jnp.full_like(conduct, SHIFT)
    for axis_id in range(3):
        for offset in (1, -1):
            total = total + 0.5 * (conduct + jnp.roll(conduct, -offset, axis_id))
    return total


def smooth_global(field, source, conduct, inverse, weights):
    change = jnp.zeros_like(field)
    for carry, weight in weights:
        resid = source - operate_global(field, conduct)
        change = carry * change + weight * inverse * resid
        field = field + change
    return field


def restrict(field):
    extent_x, extent_y, extent_z = field.shape
    return field.reshape(extent_x // 2, 2, extent_y // 2, 2, extent_z // 2, 2).mean(axis=(1, 3, 5))


def prolong(field):
    extent_x, extent_y, extent_z = field.shape
    spread = jnp.broadcast_to(
        field[:, None, :, None, :, None], (extent_x, 2, extent_y, 2, extent_z, 2)
    )
    return spread.reshape(2 * extent_x, 2 * extent_y, 2 * extent_z)


def coarse_solve(source, conduct):
    inverse = 1.0 / diagonal_global(conduct)
    weights = chebyshev_weights(COARSE_ITERS, COARSE_FLOOR)
    return smooth_global(jnp.zeros_like(source), source, conduct, inverse, weights)


def trimmed(array, margin):
    if margin == 0:
        return array
    return array[
        margin : array.shape[0] - margin,
        margin : array.shape[1] - margin,
        margin : array.shape[2] - margin,
    ]


def shifted(array, axis_id, offset):
    index = [
        slice(1, array.shape[0] - 1),
        slice(1, array.shape[1] - 1),
        slice(1, array.shape[2] - 1),
    ]
    index[axis_id] = slice(1 + offset, array.shape[axis_id] - 1 + offset)
    return array[tuple(index)]


def operate_padded(field, conduct):
    centre = trimmed(field, 1)
    middle = trimmed(conduct, 1)
    total = SHIFT * centre
    for axis_id in range(3):
        for offset in (1, -1):
            face = 0.5 * (middle + shifted(conduct, axis_id, offset))
            total = total + face * (centre - shifted(field, axis_id, offset))
    return total


def diagonal_padded(conduct):
    middle = trimmed(conduct, 1)
    total = jnp.full_like(middle, SHIFT)
    for axis_id in range(3):
        for offset in (1, -1):
            total = total + 0.5 * (middle + shifted(conduct, axis_id, offset))
    return total


def assemble(gathered, block):
    grid_x, grid_y, grid_z = (lax.axis_size("gx"), lax.axis_size("gy"), lax.axis_size("gz"))
    block_x, block_y, block_z = block
    pieces = gathered.reshape(2, grid_x, grid_y, grid_z, block_x, block_y, block_z)
    return pieces.transpose(0, 1, 4, 2, 5, 3, 6).reshape(
        2, grid_x * block_x, grid_y * block_y, grid_z * block_z
    )


def own_block(whole, block):
    block_x, block_y, block_z = block
    corner = (
        lax.axis_index("gx") * block_x,
        lax.axis_index("gy") * block_y,
        lax.axis_index("gz") * block_z,
    )
    return lax.dynamic_slice(whole, corner, block)


def level_cycle(level, source, conduct, start):
    width = 1
    rim_input = conduct[None]
    padded = extended(rim_input, (("gx", 1), ("gy", 2), ("gz", 3)), width)
    conduct_pad = padded[0]
    inverse_pad = 1.0 / diagonal_padded(conduct_pad)
    weights = chebyshev_weights(DEG, SMOOTH_FLOOR)

    def source_at():
        return source

    def smooth_block(field, zero_start):
        change = jnp.zeros_like(field)
        position = 0
        if zero_start:
            change = weights[0][1] * trimmed(inverse_pad, width - 1) * source
            field = change
            position = 1
        while position < len(weights):
            count = min(width, len(weights) - position)
            both = extended(jnp.stack([field, change]), (("gx", 1), ("gy", 2), ("gz", 3)), count)
            field_pad = both[0]
            change_pad = both[1]
            resid = source_at() - operate_padded(field_pad, trimmed(conduct_pad, width - count))
            carry, weight = weights[position]
            change_pad = (
                carry * trimmed(change_pad, 1)
                + weight * trimmed(inverse_pad, width - count) * resid
            )
            field_pad = trimmed(field_pad, 1) + change_pad
            field = field_pad
            change = change_pad
            position = position + count
        return field

    def residual_of(field):
        rim = extended(field, (("gx", 0), ("gy", 1), ("gz", 2)), 1)
        return source - operate_padded(rim, trimmed(conduct_pad, width - 1))

    field = smooth_block(start, level > 0)
    resid = residual_of(field)
    coarse_source = restrict(resid)
    coarse_conduct = 0.25 * restrict(conduct)
    if level + 1 == LEVELS:
        gathered = lax.all_gather(
            jnp.stack([coarse_source, coarse_conduct]), ("gx", "gy", "gz"), axis=1, tiled=True
        )
        whole = assemble(gathered, coarse_source.shape)
        correction = own_block(coarse_solve(whole[0], whole[1]), coarse_source.shape)
    else:
        correction = level_cycle(
            level + 1, coarse_source, coarse_conduct, jnp.zeros_like(coarse_source)
        )
    field = smooth_block(field + prolong(correction), False)
    if level == 0:
        return (field, residual_of(field))
    return field


def per_device(source, conductance, pressure_start):
    pressure, residual = level_cycle(0, source, conductance, pressure_start)
    return (pressure, residual)


def solution(mesh):
    placed = (P("gx", "gy", "gz"), P("gx", "gy", "gz"), P("gx", "gy", "gz"))
    return jax.shard_map(
        per_device,
        mesh=mesh,
        in_specs=placed,
        out_specs=(P("gx", "gy", "gz"), P("gx", "gy", "gz")),
        check_vma=False,
    )
```

profile of v0, /device:TPU:6, one launch (start us, length us, event | category | flops | bytes accessed | tf_op | source)
XLA Modules:
  0.0 515.5 jit_solution(9670224430390955560)
XLA Ops:
  17.1 4.0 collective-permute-start.11
  27.9 8.2 %collective-permute-done.4 = f32[2,18,18,1]{3,2,1,0:T(8,128)S(1)} collective-permute-done((f32[2,18,18,1]{3,2,1,0:T(8,128)S(1)}, f32[2,18,18,1]{3,2,1,0:T(8,128)S(1)}, u32[]{:S(2)}, u32[]{:S(2)}) %collective-permute-start.4) | collective-permute-done | bytes 2624 | tf_op jit(solution)/shard_map/ppermute | solution.py:22
  46.3 3.6 collective-permute-start.17
  49.9 9.8 %reshape.83 = f32[8,2,8,2,64,2]{5,4,3,2,1,0:T(8,128)} reshape(f32[16,16,128]{2,1,0:T(8,128)S(1)} %copy-done.1) | data formatting | bytes 262144 | tf_op jit(solution)/shard_map/reshape | solution.py:72
  59.7 4.0 reduce_sum.54
  80.3 8.6 %collective-permute-done.22 = f32[2,18,18,1]{3,2,1,0:T(8,128)S(1)} collective-permute-done((f32[2,18,18,1]{3,2,1,0:T(8,128)S(1)}, f32[2,18,18,1]{3,2,1,0:T(8,128)S(1)}, u32[]{:S(2)}, u32[]{:S(2)}) %collective-permute-start.22) | collective-permute-done | bytes 2624 | tf_op jit(solution)/shard_map/ppermute | solution.py:22
  103.3 5.4 %collective-permute-done.34 = f32[18,18,1]{2,1,0:T(8,128)S(1)} collective-permute-done((f32[18,18,1]{2,1,0:T(8,128)S(1)}, f32[18,18,1]{2,1,0:T(8,128)S(1)}, u32[]{:S(2)}, u32[]{:S(2)}) %collective-permute-start.34) | collective-permute-done | bytes 1328 | tf_op jit(solution)/shard_map/ppermute | solution.py:24
  108.7 3.9 collective-permute-done.35
  112.9 9.8 %reshape.84 = f32[8,2,8,2,64,2]{5,4,3,2,1,0:T(8,128)} reshape(f32[16,16,128]{2,1,0:T(8,128)S(1)} %fusion.68) | data formatting | bytes 262144 | tf_op jit(solution)/shard_map/reshape | solution.py:72
  122.7 4.0 reduce_sum.55
  152.4 3.7 collective-permute-start.47
  175.4 3.5 collective-permute-done.59
  206.0 3.7 collective-permute-start.71
  216.5 3.5 collective-permute-done.73
  223.2 3.4 collective-permute-start.76
  228.2 3.4 collective-permute-done.77
  232.0 72.8 %all_gather.3 = f32[2,512,2,16]{3,2,1,0:T(2,128)S(1)} all-gather(f32[2,2,2,16]{3,2,1,0:T(2,128)S(1)} %pad_maximum_fusion.210), channel_id=1, replica_groups=mesh['gx'=4,'gy'=8,'gz'=8] {'gx','gy','gz'}, dimensions={1}, use_global_device_ids=true | all-gather | bytes 131584 | tf_op jit(solution)/shard_map/all_gather | solution.py:192
  411.1 3.9 broadcast_in_dim.36
  415.0 6.9 %reshape.90 = f32[16,16,128]{2,1,0:T(8,128)S(1)} reshape(f32[8,2,8,2,64,2]{5,4,3,2,1,0:T(8,128)} %broadcast_in_dim.36) | data formatting | bytes 262144 | tf_op jit(solution)/shard_map/reshape | solution.py:80
  435.1 7.9 %collective-permute-done.118 = f32[2,18,18,1]{3,2,1,0:T(8,128)S(1)} collective-permute-done((f32[2,18,18,1]{3,2,1,0:T(8,128)S(1)}, f32[2,18,18,1]{3,2,1,0:T(8,128)S(1)}, u32[]{:S(2)}, u32[]{:S(2)}) %collective-permute-start.118) | collective-permute-done | bytes 2624 | tf_op jit(solution)/shard_map/ppermute | solution.py:22
  457.5 8.2 %collective-permute-done.124 = f32[2,18,18,1]{3,2,1,0:T(8,128)S(1)} collective-permute-done((f32[2,18,18,1]{3,2,1,0:T(8,128)S(1)}, f32[2,18,18,1]{3,2,1,0:T(8,128)S(1)}, u32[]{:S(2)}, u32[]{:S(2)}) %collective-permute-start.124) | collective-permute-done | bytes 2624 | tf_op jit(solution)/shard_map/ppermute | solution.py:22
  479.6 9.1 %collective-permute-done.130 = f32[2,18,18,1]{3,2,1,0:T(8,128)S(1)} collective-permute-done((f32[2,18,18,1]{3,2,1,0:T(8,128)S(1)}, f32[2,18,18,1]{3,2,1,0:T(8,128)S(1)}, u32[]{:S(2)}, u32[]{:S(2)}) %collective-permute-start.130) | collective-permute-done | bytes 2624 | tf_op jit(solution)/shard_map/ppermute | solution.py:22
  495.5 3.5 collective-permute-done.133
  504.9 5.8 %collective-permute-done.136 = f32[18,18,1]{2,1,0:T(8,128)S(1)} collective-permute-done((f32[18,18,1]{2,1,0:T(8,128)S(1)}, f32[18,18,1]{2,1,0:T(8,128)S(1)}, u32[]{:S(2)}, u32[]{:S(2)}) %collective-permute-start.136) | collective-permute-done | bytes 1328 | tf_op jit(solution)/shard_map/ppermute | solution.py:24
  (534 shorter events, 312.0 us)
Async XLA Ops:
  1.4 8.1 %collective-permute-start.6 = (f32[1,1,16,128]{3,2,1,0:T(8,128)S(1)}, f32[1,1,16,128]{3,2,1,0:T(8,128)S(1)}, u32[]{:S(2)}, u32[]{:S(2)}) collective-permute-start(f32[1,1,16,128]{3,2,1,0:T(8,128)S(1)} %get-tuple-element.153), channel_id=1, source_target_pairs={{0,64},{64,128},{128,192},{192,0},{1,65},{65,129},{129,193},{193,1... | collective-permute-start | bytes 24584 | tf_op jit(solution)/shard_map/ppermute | solution.py:22
  12.2 8.9 %collective-permute-start.2 = (f32[2,18,1,128]{3,2,1,0:T(1,128)S(1)}, f32[2,18,1,128]{3,2,1,0:T(1,128)S(1)}, u32[]{:S(2)}, u32[]{:S(2)}) collective-permute-start(f32[2,18,1,128]{3,2,1,0:T(1,128)S(1)} %get-tuple-element.105), channel_id=1, source_target_pairs={{0,8},{8,16},{16,24},{24,32},{32,40},{40,48},{48,56},{56,0},{1,9},... | collective-permute-start | bytes 55304 | tf_op jit(solution)/shard_map/ppermute | solution.py:22
  12.9 8.3 %collective-permute-start.3 = (f32[2,18,1,128]{3,2,1,0:T(1,128)S(1)}, f32[2,18,1,128]{3,2,1,0:T(1,128)S(1)}, u32[]{:S(2)}, u32[]{:S(2)}) collective-permute-start(f32[2,18,1,128]{3,2,1,0:T(1,128)S(1)} %get-tuple-element.106), channel_id=1, source_target_pairs={{8,0},{16,8},{24,16},{32,24},{40,32},{48,40},{56,48},{0,56},{9,1},... | collective-permute-start | bytes 55304 | tf_op jit(solution)/shard_map/ppermute | solution.py:24
  15.1 11.6 %collective-permute-start.10 = (f32[1,18,18,1]{3,2,1,0:T(8,128)S(1)}, f32[1,18,18,1]{3,2,1,0:T(8,128)S(1)}, u32[]{:S(2)}, u32[]{:S(2)}) collective-permute-start(f32[1,18,18,1]{3,2,1,0:T(8,128)S(1)} %get-tuple-element.119), channel_id=1, source_target_pairs={{0,1},{1,2},{2,3},{3,4},{4,5},{5,6},{6,7},{7,0},{8,9},{9,10},{10,1... | collective-permute-start | bytes 3896 | tf_op jit(solution)/shard_map/ppermute | solution.py:22
  17.1 9.6 %collective-permute-start.11 = (f32[1,18,18,1]{3,2,1,0:T(8,128)S(1)}, f32[1,18,18,1]{3,2,1,0:T(8,128)S(1)}, u32[]{:S(2)}, u32[]{:S(2)}) collective-permute-start(f32[1,18,18,1]{3,2,1,0:T(8,128)S(1)} %get-tuple-element.120), channel_id=1, source_target_pairs={{1,0},{2,1},{3,2},{4,3},{5,4},{6,5},{7,6},{0,7},{9,8},{10,9},{11,1... | collective-permute-start | bytes 3896 | tf_op jit(solution)/shard_map/ppermute | solution.py:24
  21.4 14.8 %collective-permute-start.4 = (f32[2,18,18,1]{3,2,1,0:T(8,128)S(1)}, f32[2,18,18,1]{3,2,1,0:T(8,128)S(1)}, u32[]{:S(2)}, u32[]{:S(2)}) collective-permute-start(f32[2,18,18,1]{3,2,1,0:T(8,128)S(1)} %get-tuple-element.93), channel_id=1, source_target_pairs={{0,1},{1,2},{2,3},{3,4},{4,5},{5,6},{6,7},{7,0},{8,9},{9,10},{10,1... | collective-permute-start | bytes 7784 | tf_op jit(solution)/shard_map/ppermute | solution.py:22
  21.5 14.7 %collective-permute-start.5 = (f32[2,18,18,1]{3,2,1,0:T(8,128)S(1)}, f32[2,18,18,1]{3,2,1,0:T(8,128)S(1)}, u32[]{:S(2)}, u32[]{:S(2)}) collective-permute-start(f32[2,18,18,1]{3,2,1,0:T(8,128)S(1)} %get-tuple-element.94), channel_id=1, source_target_pairs={{1,0},{2,1},{3,2},{4,3},{5,4},{6,5},{7,6},{0,7},{9,8},{10,9},{11,1... | collective-permute-start | bytes 7784 | tf_op jit(solution)/shard_map/ppermute | solution.py:24
  45.9 17.8 %collective-permute-start.16 = (f32[2,18,18,1]{3,2,1,0:T(8,128)S(1)}, f32[2,18,18,1]{3,2,1,0:T(8,128)S(1)}, u32[]{:S(2)}, u32[]{:S(2)}) collective-permute-start(f32[2,18,18,1]{3,2,1,0:T(8,128)S(1)} %get-tuple-element.91), channel_id=1, source_target_pairs={{0,1},{1,2},{2,3},{3,4},{4,5},{5,6},{6,7},{7,0},{8,9},{9,10},{10,1... | collective-permute-start | bytes 7784 | tf_op jit(solution)/shard_map/ppermute | solution.py:22
  46.3 17.4 %collective-permute-start.17 = (f32[2,18,18,1]{3,2,1,0:T(8,128)S(1)}, f32[2,18,18,1]{3,2,1,0:T(8,128)S(1)}, u32[]{:S(2)}, u32[]{:S(2)}) collective-permute-start(f32[2,18,18,1]{3,2,1,0:T(8,128)S(1)} %get-tuple-element.92), channel_id=1, source_target_pairs={{1,0},{2,1},{3,2},{4,3},{5,4},{6,5},{7,6},{0,7},{9,8},{10,9},{11,1... | collective-permute-start | bytes 7784 | tf_op jit(solution)/shard_map/ppermute | solution.py:24
  75.2 13.7 %collective-permute-start.22 = (f32[2,18,18,1]{3,2,1,0:T(8,128)S(1)}, f32[2,18,18,1]{3,2,1,0:T(8,128)S(1)}, u32[]{:S(2)}, u32[]{:S(2)}) collective-permute-start(f32[2,18,18,1]{3,2,1,0:T(8,128)S(1)} %get-tuple-element.89), channel_id=1, source_target_pairs={{0,1},{1,2},{2,3},{3,4},{4,5},{5,6},{6,7},{7,0},{8,9},{9,10},{10,1... | collective-permute-start | bytes 7784 | tf_op jit(solution)/shard_map/ppermute | solution.py:22
  75.3 13.8 %collective-permute-start.23 = (f32[2,18,18,1]{3,2,1,0:T(8,128)S(1)}, f32[2,18,18,1]{3,2,1,0:T(8,128)S(1)}, u32[]{:S(2)}, u32[]{:S(2)}) collective-permute-start(f32[2,18,18,1]{3,2,1,0:T(8,128)S(1)} %get-tuple-element.90), channel_id=1, source_target_pairs={{1,0},{2,1},{3,2},{4,3},{5,4},{6,5},{7,6},{0,7},{9,8},{10,9},{11,1... | collective-permute-start | bytes 7784 | tf_op jit(solution)/shard_map/ppermute | solution.py:24
  78.5 13.6 %collective-permute-start.26 = (f32[1,10,1,64]{3,2,1,0:T(1,128)S(1)}, f32[1,10,1,64]{3,2,1,0:T(1,128)S(1)}, u32[]{:S(2)}, u32[]{:S(2)}) collective-permute-start(f32[1,10,1,64]{3,2,1,0:T(1,128)S(1)} %get-tuple-element.346), channel_id=1, source_target_pairs={{0,8},{8,16},{16,24},{24,32},{32,40},{40,48},{48,56},{56,0},{1,9},... | collective-permute-start | bytes 7688 | tf_op jit(solution)/shard_map/ppermute | solution.py:22
  79.6 12.5 %collective-permute-start.27 = (f32[1,10,1,64]{3,2,1,0:T(1,128)S(1)}, f32[1,10,1,64]{3,2,1,0:T(1,128)S(1)}, u32[]{:S(2)}, u32[]{:S(2)}) collective-permute-start(f32[1,10,1,64]{3,2,1,0:T(1,128)S(1)} %get-tuple-element.347), channel_id=1, source_target_pairs={{8,0},{16,8},{24,16},{32,24},{40,32},{48,40},{56,48},{0,56},{9,1},... | collective-permute-start | bytes 7688 | tf_op jit(solution)/shard_map/ppermute | solution.py:24
  99.9 8.9 %collective-permute-start.34 = (f32[18,18,1]{2,1,0:T(8,128)S(1)}, f32[18,18,1]{2,1,0:T(8,128)S(1)}, u32[]{:S(2)}, u32[]{:S(2)}) collective-permute-start(f32[18,18,1]{2,1,0:T(8,128)S(1)} %get-tuple-element.117), channel_id=1, source_target_pairs={{1,0},{2,1},{3,2},{4,3},{5,4},{6,5},{7,6},{0,7},{9,8},{10,9},{11,1... | collective-permute-start | bytes 3896 | tf_op jit(solution)/shard_map/ppermute | solution.py:24
  103.2 9.5 %collective-permute-start.35 = (f32[18,18,1]{2,1,0:T(8,128)S(1)}, f32[18,18,1]{2,1,0:T(8,128)S(1)}, u32[]{:S(2)}, u32[]{:S(2)}) collective-permute-start(f32[18,18,1]{2,1,0:T(8,128)S(1)} %get-tuple-element.118), channel_id=1, source_target_pairs={{0,1},{1,2},{2,3},{3,4},{4,5},{5,6},{6,7},{7,0},{8,9},{9,10},{10,1... | collective-permute-start | bytes 3896 | tf_op jit(solution)/shard_map/ppermute | solution.py:22
  152.4 7.5 %collective-permute-start.47 = (f32[2,10,10,1]{3,2,1,0:T(8,128)S(1)}, f32[2,10,10,1]{3,2,1,0:T(8,128)S(1)}, u32[]{:S(2)}, u32[]{:S(2)}) collective-permute-start(f32[2,10,10,1]{3,2,1,0:T(8,128)S(1)} %get-tuple-element.136), channel_id=1, source_target_pairs={{1,0},{2,1},{3,2},{4,3},{5,4},{6,5},{7,6},{0,7},{9,8},{10,9},{11,1... | collective-permute-start | bytes 2408 | tf_op jit(solution)/shard_map/ppermute | solution.py:24
  431.7 11.3 %collective-permute-start.118 = (f32[2,18,18,1]{3,2,1,0:T(8,128)S(1)}, f32[2,18,18,1]{3,2,1,0:T(8,128)S(1)}, u32[]{:S(2)}, u32[]{:S(2)}) collective-permute-start(f32[2,18,18,1]{3,2,1,0:T(8,128)S(1)} %get-tuple-element.87), channel_id=1, source_target_pairs={{0,1},{1,2},{2,3},{3,4},{4,5},{5,6},{6,7},{7,0},{8,9},{9,10},{10,1... | collective-permute-start | bytes 7784 | tf_op jit(solution)/shard_map/ppermute | solution.py:22
  433.1 10.5 %collective-permute-start.119 = (f32[2,18,18,1]{3,2,1,0:T(8,128)S(1)}, f32[2,18,18,1]{3,2,1,0:T(8,128)S(1)}, u32[]{:S(2)}, u32[]{:S(2)}) collective-permute-start(f32[2,18,18,1]{3,2,1,0:T(8,128)S(1)} %get-tuple-element.88), channel_id=1, source_target_pairs={{1,0},{2,1},{3,2},{4,3},{5,4},{6,5},{7,6},{0,7},{9,8},{10,9},{11,1... | collective-permute-start | bytes 7784 | tf_op jit(solution)/shard_map/ppermute | solution.py:24
  453.9 11.8 %collective-permute-start.124 = (f32[2,18,18,1]{3,2,1,0:T(8,128)S(1)}, f32[2,18,18,1]{3,2,1,0:T(8,128)S(1)}, u32[]{:S(2)}, u32[]{:S(2)}) collective-permute-start(f32[2,18,18,1]{3,2,1,0:T(8,128)S(1)} %get-tuple-element.85), channel_id=1, source_target_pairs={{0,1},{1,2},{2,3},{3,4},{4,5},{5,6},{6,7},{7,0},{8,9},{9,10},{10,1... | collective-permute-start | bytes 7784 | tf_op jit(solution)/shard_map/ppermute | solution.py:22
  455.5 11.1 %collective-permute-start.125 = (f32[2,18,18,1]{3,2,1,0:T(8,128)S(1)}, f32[2,18,18,1]{3,2,1,0:T(8,128)S(1)}, u32[]{:S(2)}, u32[]{:S(2)}) collective-permute-start(f32[2,18,18,1]{3,2,1,0:T(8,128)S(1)} %get-tuple-element.86), channel_id=1, source_target_pairs={{1,0},{2,1},{3,2},{4,3},{5,4},{6,5},{7,6},{0,7},{9,8},{10,9},{11,1... | collective-permute-start | bytes 7784 | tf_op jit(solution)/shard_map/ppermute | solution.py:24
  476.3 12.4 %collective-permute-start.130 = (f32[2,18,18,1]{3,2,1,0:T(8,128)S(1)}, f32[2,18,18,1]{3,2,1,0:T(8,128)S(1)}, u32[]{:S(2)}, u32[]{:S(2)}) collective-permute-start(f32[2,18,18,1]{3,2,1,0:T(8,128)S(1)} %get-tuple-element.83), channel_id=1, source_target_pairs={{0,1},{1,2},{2,3},{3,4},{4,5},{5,6},{6,7},{7,0},{8,9},{9,10},{10,1... | collective-permute-start | bytes 7784 | tf_op jit(solution)/shard_map/ppermute | solution.py:22
  477.6 12.2 %collective-permute-start.131 = (f32[2,18,18,1]{3,2,1,0:T(8,128)S(1)}, f32[2,18,18,1]{3,2,1,0:T(8,128)S(1)}, u32[]{:S(2)}, u32[]{:S(2)}) collective-permute-start(f32[2,18,18,1]{3,2,1,0:T(8,128)S(1)} %get-tuple-element.84), channel_id=1, source_target_pairs={{1,0},{2,1},{3,2},{4,3},{5,4},{6,5},{7,6},{0,7},{9,8},{10,9},{11,1... | collective-permute-start | bytes 7784 | tf_op jit(solution)/shard_map/ppermute | solution.py:24
  502.3 8.5 %collective-permute-start.136 = (f32[18,18,1]{2,1,0:T(8,128)S(1)}, f32[18,18,1]{2,1,0:T(8,128)S(1)}, u32[]{:S(2)}, u32[]{:S(2)}) collective-permute-start(f32[18,18,1]{2,1,0:T(8,128)S(1)} %get-tuple-element.115), channel_id=1, source_target_pairs={{1,0},{2,1},{3,2},{4,3},{5,4},{6,5},{7,6},{0,7},{9,8},{10,9},{11,1... | collective-permute-start | bytes 3896 | tf_op jit(solution)/shard_map/ppermute | solution.py:24
  504.9 9.2 %collective-permute-start.137 = (f32[18,18,1]{2,1,0:T(8,128)S(1)}, f32[18,18,1]{2,1,0:T(8,128)S(1)}, u32[]{:S(2)}, u32[]{:S(2)}) collective-permute-start(f32[18,18,1]{2,1,0:T(8,128)S(1)} %get-tuple-element.116), channel_id=1, source_target_pairs={{0,1},{1,2},{2,3},{3,4},{4,5},{5,6},{6,7},{7,0},{8,9},{9,10},{10,1... | collective-permute-start | bytes 3896 | tf_op jit(solution)/shard_map/ppermute | solution.py:22
  (117 other events, 624.3 us)
where the time goes:
time: 524 us; the launch traced here: 515 us
  starting transfers between devices  191 us (36%)
  waiting for transfers between devices  182 us (35%)
  blocking collectives  72.8 us (14%)
  local copies, waits for them, and re-layouts  42.4 us (8%)
  other arithmetic  25.1 us (5%)
    ppermute x69, waiting for transfers between devices, extended(): lax.ppermute(tail, axis, [(i, (i + 1) % count) for i in range(count)])  137 us
    ppermute x69, starting transfers between devices, extended(): lax.ppermute(head, axis, [((i + 1) % count, i) for i in range(count)])  130 us
    all_gather x1, blocking collectives, level_cycle(): lax.all_gather(jnp.stack([coarse_source, coarse_conduct]), ('gx', 'gy', '...  72.8 us
    ppermute x69, starting transfers between devices, extended(): lax.ppermute(tail, axis, [(i, (i + 1) % count) for i in range(count)])  60.4 us
    ppermute x69, waiting for transfers between devices, extended(): lax.ppermute(head, axis, [((i + 1) % count, i) for i in range(count)])  44.6 us
    reshape x4, local copies, waits for them, and re-layouts, restrict(): field.reshape(extent_x // 2, 2, extent_y // 2, 2, extent_z // 2, 2)  20.8 us
  transfers between devices with their start and end apart: 138, of which 92 were waited for; matrix products, arithmetic and copies ran while one was open for 4% of the time, Pallas kernels for 0%

commit v1 on v0

--- a/solution.py
+++ b/solution.py
@@ -189,8 +189,16 @@
     coarse_source = restrict(resid)
     coarse_conduct = 0.25 * restrict(conduct)
     if level + 1 == LEVELS:
-        gathered = lax.all_gather(
-            jnp.stack([coarse_source, coarse_conduct]), ("gx", "gy", "gz"), axis=1, tiled=True
+        gathered = jnp.concatenate(
+            lax.all_to_all(
+                jnp.stack(
+                    [jnp.stack([coarse_source, coarse_conduct])] * lax.axis_size(("gx", "gy", "gz"))
+                ),
+                ("gx", "gy", "gz"),
+                0,
+                0,
+            ),
+            axis=1,
         )
         whole = assemble(gathered, coarse_source.shape)
         correction = own_block(coarse_solve(whole[0], whole[1]), coarse_source.shape)

time: 524 us -> 476 us (0.908)
  blocking collectives: 72.8 us -> 0 us
  starting transfers between devices: 191 us -> 204 us
    all_gather x1 -> x0, blocking collectives: 72.8 us -> none  [level_cycle(): lax.all_gather(jnp.stack([coarse_source, coarse_conduct]), ('gx', 'gy', '...]
    all_to_all x0 -> x1, starting transfers between devices: none -> 11.6 us  [level_cycle(): lax.all_to_all(jnp.stack([jnp.stack([coarse_source, coarse_conduct])] * l...]
    all_to_all x0 -> x1, waiting for transfers between devices: none -> 10.9 us  [level_cycle(): lax.all_to_all(jnp.stack([jnp.stack([coarse_source, coarse_conduct])] * l...]
    ppermute x69, waiting for transfers between devices: 44.6 us -> 39.2 us  [extended(): lax.ppermute(head, axis, [((i + 1) % count, i) for i in range(count)])]
  transfers between devices with their start and end apart: 138 -> 139, of which waited for: 92 -> 90; matrix products, arithmetic and copies ran while one was open for 4% -> 5% of each run, Pallas kernels for 0% -> 0%
where the time goes in v1:
time: 476 us; the launch traced here: 467 us
  starting transfers between devices  204 us (43%)
  waiting for transfers between devices  187 us (39%)
  local copies, waits for them, and re-layouts  46.8 us (10%)
  other arithmetic  26.1 us (5%)
    ppermute x69, waiting for transfers between devices, extended(): lax.ppermute(tail, axis, [(i, (i + 1) % count) for i in range(count)])  137 us
    ppermute x69, starting transfers between devices, extended(): lax.ppermute(head, axis, [((i + 1) % count, i) for i in range(count)])  134 us
    ppermute x69, starting transfers between devices, extended(): lax.ppermute(tail, axis, [(i, (i + 1) % count) for i in range(count)])  58.7 us
    ppermute x69, waiting for transfers between devices, extended(): lax.ppermute(head, axis, [((i + 1) % count, i) for i in range(count)])  39.2 us
    reshape x4, local copies, waits for them, and re-layouts, restrict(): field.reshape(extent_x // 2, 2, extent_y // 2, 2, extent_z // 2, 2)  20.8 us
    all_to_all x1, starting transfers between devices, level_cycle(): lax.all_to_all(jnp.stack([jnp.stack([coarse_source, coarse_conduct])] * l...  11.6 us
    all_to_all x1, waiting for transfers between devices, level_cycle(): lax.all_to_all(jnp.stack([jnp.stack([coarse_source, coarse_conduct])] * l...  10.9 us
  transfers between devices with their start and end apart: 139, of which 90 were waited for; matrix products, arithmetic and copies ran while one was open for 5% of the time, Pallas kernels for 0%

profile of v1, /device:TPU:6, one launch (start us, length us, event | category | flops | bytes accessed | tf_op | source)
XLA Modules:
  0.0 466.7 jit_solution(15401812013884554435)
XLA Ops:
  17.1 4.0 collective-permute-start.11
  27.9 8.2 %collective-permute-done.4 = f32[2,18,18,1]{3,2,1,0:T(8,128)S(1)} collective-permute-done((f32[2,18,18,1]{3,2,1,0:T(8,128)S(1)}, f32[2,18,18,1]{3,2,1,0:T(8,128)S(1)}, u32[]{:S(2)}, u32[]{:S(2)}) %collective-permute-start.4) | collective-permute-done | bytes 2624 | tf_op jit(solution)/shard_map/ppermute | solution.py:22
  46.3 3.6 collective-permute-start.17
  49.9 9.8 %reshape.85 = f32[8,2,8,2,64,2]{5,4,3,2,1,0:T(8,128)} reshape(f32[16,16,128]{2,1,0:T(8,128)S(1)} %copy-done.1) | data formatting | bytes 262144 | tf_op jit(solution)/shard_map/reshape | solution.py:72
  59.7 4.0 reduce_sum.54
  80.2 8.6 %collective-permute-done.22 = f32[2,18,18,1]{3,2,1,0:T(8,128)S(1)} collective-permute-done((f32[2,18,18,1]{3,2,1,0:T(8,128)S(1)}, f32[2,18,18,1]{3,2,1,0:T(8,128)S(1)}, u32[]{:S(2)}, u32[]{:S(2)}) %collective-permute-start.22) | collective-permute-done | bytes 2624 | tf_op jit(solution)/shard_map/ppermute | solution.py:22
  103.2 5.4 %collective-permute-done.34 = f32[18,18,1]{2,1,0:T(8,128)S(1)} collective-permute-done((f32[18,18,1]{2,1,0:T(8,128)S(1)}, f32[18,18,1]{2,1,0:T(8,128)S(1)}, u32[]{:S(2)}, u32[]{:S(2)}) %collective-permute-start.34) | collective-permute-done | bytes 1328 | tf_op jit(solution)/shard_map/ppermute | solution.py:24
  108.6 3.9 collective-permute-done.35
  112.8 9.8 %reshape.86 = f32[8,2,8,2,64,2]{5,4,3,2,1,0:T(8,128)} reshape(f32[16,16,128]{2,1,0:T(8,128)S(1)} %fusion.68) | data formatting | bytes 262144 | tf_op jit(solution)/shard_map/reshape | solution.py:72
  122.6 4.0 reduce_sum.55
  152.3 3.7 collective-permute-start.47
  175.3 3.5 collective-permute-done.59
  205.9 3.7 collective-permute-start.71
  216.4 3.5 collective-permute-done.73
  234.3 11.6 %all-to-all-start = ((f32[256,1,128]{2,1,0:T(1,128)}), f32[256,1,128]{2,1,0:T(1,128)S(1)}, u32[]{:S(2)}, u32[]{:S(2)}) async-start(f32[256,1,128]{2,1,0:T(1,128)} %reshape.93), calls=%async_computation | async-start | bytes 262144 | tf_op jit(solution)/shard_map/all_to_all | solution.py:193
  246.0 10.9 %all-to-all-done = f32[256,1,128]{2,1,0:T(1,128)S(1)} async-done(((f32[256,1,128]{2,1,0:T(1,128)}), f32[256,1,128]{2,1,0:T(1,128)S(1)}, u32[]{:S(2)}, u32[]{:S(2)}) %all-to-all-start) | async-done | bytes 131104 | tf_op jit(solution)/shard_map/all_to_all | solution.py:193
  361.7 3.9 broadcast_in_dim.36
  365.6 6.9 %reshape.92 = f32[16,16,128]{2,1,0:T(8,128)S(1)} reshape(f32[8,2,8,2,64,2]{5,4,3,2,1,0:T(8,128)} %broadcast_in_dim.36) | data formatting | bytes 262144 | tf_op jit(solution)/shard_map/reshape | solution.py:80
  385.9 7.8 %collective-permute-done.118 = f32[2,18,18,1]{3,2,1,0:T(8,128)S(1)} collective-permute-done((f32[2,18,18,1]{3,2,1,0:T(8,128)S(1)}, f32[2,18,18,1]{3,2,1,0:T(8,128)S(1)}, u32[]{:S(2)}, u32[]{:S(2)}) %collective-permute-start.118) | collective-permute-done | bytes 2624 | tf_op jit(solution)/shard_map/ppermute | solution.py:22
  408.4 8.2 %collective-permute-done.124 = f32[2,18,18,1]{3,2,1,0:T(8,128)S(1)} collective-permute-done((f32[2,18,18,1]{3,2,1,0:T(8,128)S(1)}, f32[2,18,18,1]{3,2,1,0:T(8,128)S(1)}, u32[]{:S(2)}, u32[]{:S(2)}) %collective-permute-start.124) | collective-permute-done | bytes 2624 | tf_op jit(solution)/shard_map/ppermute | solution.py:22
  431.8 8.2 %collective-permute-done.130 = f32[2,18,18,1]{3,2,1,0:T(8,128)S(1)} collective-permute-done((f32[2,18,18,1]{3,2,1,0:T(8,128)S(1)}, f32[2,18,18,1]{3,2,1,0:T(8,128)S(1)}, u32[]{:S(2)}, u32[]{:S(2)}) %collective-permute-start.130) | collective-permute-done | bytes 2624 | tf_op jit(solution)/shard_map/ppermute | solution.py:22
  445.7 3.5 collective-permute-done.133
  456.9 4.7 %collective-permute-done.136 = f32[18,18,1]{2,1,0:T(8,128)S(1)} collective-permute-done((f32[18,18,1]{2,1,0:T(8,128)S(1)}, f32[18,18,1]{2,1,0:T(8,128)S(1)}, u32[]{:S(2)}, u32[]{:S(2)}) %collective-permute-start.136) | collective-permute-done | bytes 1328 | tf_op jit(solution)/shard_map/ppermute | solution.py:24
  461.6 4.0 collective-permute-done.137
  (542 shorter events, 318.5 us)
Async XLA Ops:
  1.4 8.1 %collective-permute-start.6 = (f32[1,1,16,128]{3,2,1,0:T(8,128)S(1)}, f32[1,1,16,128]{3,2,1,0:T(8,128)S(1)}, u32[]{:S(2)}, u32[]{:S(2)}) collective-permute-start(f32[1,1,16,128]{3,2,1,0:T(8,128)S(1)} %get-tuple-element.153), channel_id=1, source_target_pairs={{0,64},{64,128},{128,192},{192,0},{1,65},{65,129},{129,193},{193,1... | collective-permute-start | bytes 24584 | tf_op jit(solution)/shard_map/ppermute | solution.py:22
  12.2 8.9 %collective-permute-start.2 = (f32[2,18,1,128]{3,2,1,0:T(1,128)S(1)}, f32[2,18,1,128]{3,2,1,0:T(1,128)S(1)}, u32[]{:S(2)}, u32[]{:S(2)}) collective-permute-start(f32[2,18,1,128]{3,2,1,0:T(1,128)S(1)} %get-tuple-element.105), channel_id=1, source_target_pairs={{0,8},{8,16},{16,24},{24,32},{32,40},{40,48},{48,56},{56,0},{1,9},... | collective-permute-start | bytes 55304 | tf_op jit(solution)/shard_map/ppermute | solution.py:22
  12.9 8.3 %collective-permute-start.3 = (f32[2,18,1,128]{3,2,1,0:T(1,128)S(1)}, f32[2,18,1,128]{3,2,1,0:T(1,128)S(1)}, u32[]{:S(2)}, u32[]{:S(2)}) collective-permute-start(f32[2,18,1,128]{3,2,1,0:T(1,128)S(1)} %get-tuple-element.106), channel_id=1, source_target_pairs={{8,0},{16,8},{24,16},{32,24},{40,32},{48,40},{56,48},{0,56},{9,1},... | collective-permute-start | bytes 55304 | tf_op jit(solution)/shard_map/ppermute | solution.py:24
  15.1 11.6 %collective-permute-start.10 = (f32[1,18,18,1]{3,2,1,0:T(8,128)S(1)}, f32[1,18,18,1]{3,2,1,0:T(8,128)S(1)}, u32[]{:S(2)}, u32[]{:S(2)}) collective-permute-start(f32[1,18,18,1]{3,2,1,0:T(8,128)S(1)} %get-tuple-element.119), channel_id=1, source_target_pairs={{0,1},{1,2},{2,3},{3,4},{4,5},{5,6},{6,7},{7,0},{8,9},{9,10},{10,1... | collective-permute-start | bytes 3896 | tf_op jit(solution)/shard_map/ppermute | solution.py:22
  17.1 9.6 %collective-permute-start.11 = (f32[1,18,18,1]{3,2,1,0:T(8,128)S(1)}, f32[1,18,18,1]{3,2,1,0:T(8,128)S(1)}, u32[]{:S(2)}, u32[]{:S(2)}) collective-permute-start(f32[1,18,18,1]{3,2,1,0:T(8,128)S(1)} %get-tuple-element.120), channel_id=1, source_target_pairs={{1,0},{2,1},{3,2},{4,3},{5,4},{6,5},{7,6},{0,7},{9,8},{10,9},{11,1... | collective-permute-start | bytes 3896 | tf_op jit(solution)/shard_map/ppermute | solution.py:24
  21.4 14.8 %collective-permute-start.4 = (f32[2,18,18,1]{3,2,1,0:T(8,128)S(1)}, f32[2,18,18,1]{3,2,1,0:T(8,128)S(1)}, u32[]{:S(2)}, u32[]{:S(2)}) collective-permute-start(f32[2,18,18,1]{3,2,1,0:T(8,128)S(1)} %get-tuple-element.93), channel_id=1, source_target_pairs={{0,1},{1,2},{2,3},{3,4},{4,5},{5,6},{6,7},{7,0},{8,9},{9,10},{10,1... | collective-permute-start | bytes 7784 | tf_op jit(solution)/shard_map/ppermute | solution.py:22
  21.5 14.7 %collective-permute-start.5 = (f32[2,18,18,1]{3,2,1,0:T(8,128)S(1)}, f32[2,18,18,1]{3,2,1,0:T(8,128)S(1)}, u32[]{:S(2)}, u32[]{:S(2)}) collective-permute-start(f32[2,18,18,1]{3,2,1,0:T(8,128)S(1)} %get-tuple-element.94), channel_id=1, source_target_pairs={{1,0},{2,1},{3,2},{4,3},{5,4},{6,5},{7,6},{0,7},{9,8},{10,9},{11,1... | collective-permute-start | bytes 7784 | tf_op jit(solution)/shard_map/ppermute | solution.py:24
  45.9 17.8 %collective-permute-start.16 = (f32[2,18,18,1]{3,2,1,0:T(8,128)S(1)}, f32[2,18,18,1]{3,2,1,0:T(8,128)S(1)}, u32[]{:S(2)}, u32[]{:S(2)}) collective-permute-start(f32[2,18,18,1]{3,2,1,0:T(8,128)S(1)} %get-tuple-element.91), channel_id=1, source_target_pairs={{0,1},{1,2},{2,3},{3,4},{4,5},{5,6},{6,7},{7,0},{8,9},{9,10},{10,1... | collective-permute-start | bytes 7784 | tf_op jit(solution)/shard_map/ppermute | solution.py:22
  46.3 17.4 %collective-permute-start.17 = (f32[2,18,18,1]{3,2,1,0:T(8,128)S(1)}, f32[2,18,18,1]{3,2,1,0:T(8,128)S(1)}, u32[]{:S(2)}, u32[]{:S(2)}) collective-permute-start(f32[2,18,18,1]{3,2,1,0:T(8,128)S(1)} %get-tuple-element.92), channel_id=1, source_target_pairs={{1,0},{2,1},{3,2},{4,3},{5,4},{6,5},{7,6},{0,7},{9,8},{10,9},{11,1... | collective-permute-start | bytes 7784 | tf_op jit(solution)/shard_map/ppermute | solution.py:24
  75.1 13.7 %collective-permute-start.22 = (f32[2,18,18,1]{3,2,1,0:T(8,128)S(1)}, f32[2,18,18,1]{3,2,1,0:T(8,128)S(1)}, u32[]{:S(2)}, u32[]{:S(2)}) collective-permute-start(f32[2,18,18,1]{3,2,1,0:T(8,128)S(1)} %get-tuple-element.89), channel_id=1, source_target_pairs={{0,1},{1,2},{2,3},{3,4},{4,5},{5,6},{6,7},{7,0},{8,9},{9,10},{10,1... | collective-permute-start | bytes 7784 | tf_op jit(solution)/shard_map/ppermute | solution.py:22
  75.2 13.8 %collective-permute-start.23 = (f32[2,18,18,1]{3,2,1,0:T(8,128)S(1)}, f32[2,18,18,1]{3,2,1,0:T(8,128)S(1)}, u32[]{:S(2)}, u32[]{:S(2)}) collective-permute-start(f32[2,18,18,1]{3,2,1,0:T(8,128)S(1)} %get-tuple-element.90), channel_id=1, source_target_pairs={{1,0},{2,1},{3,2},{4,3},{5,4},{6,5},{7,6},{0,7},{9,8},{10,9},{11,1... | collective-permute-start | bytes 7784 | tf_op jit(solution)/shard_map/ppermute | solution.py:24
  78.5 13.6 %collective-permute-start.26 = (f32[1,10,1,64]{3,2,1,0:T(1,128)S(1)}, f32[1,10,1,64]{3,2,1,0:T(1,128)S(1)}, u32[]{:S(2)}, u32[]{:S(2)}) collective-permute-start(f32[1,10,1,64]{3,2,1,0:T(1,128)S(1)} %get-tuple-element.346), channel_id=1, source_target_pairs={{0,8},{8,16},{16,24},{24,32},{32,40},{40,48},{48,56},{56,0},{1,9},... | collective-permute-start | bytes 7688 | tf_op jit(solution)/shard_map/ppermute | solution.py:22
  79.6 12.5 %collective-permute-start.27 = (f32[1,10,1,64]{3,2,1,0:T(1,128)S(1)}, f32[1,10,1,64]{3,2,1,0:T(1,128)S(1)}, u32[]{:S(2)}, u32[]{:S(2)}) collective-permute-start(f32[1,10,1,64]{3,2,1,0:T(1,128)S(1)} %get-tuple-element.347), channel_id=1, source_target_pairs={{8,0},{16,8},{24,16},{32,24},{40,32},{48,40},{56,48},{0,56},{9,1},... | collective-permute-start | bytes 7688 | tf_op jit(solution)/shard_map/ppermute | solution.py:24
  99.8 8.8 %collective-permute-start.34 = (f32[18,18,1]{2,1,0:T(8,128)S(1)}, f32[18,18,1]{2,1,0:T(8,128)S(1)}, u32[]{:S(2)}, u32[]{:S(2)}) collective-permute-start(f32[18,18,1]{2,1,0:T(8,128)S(1)} %get-tuple-element.117), channel_id=1, source_target_pairs={{1,0},{2,1},{3,2},{4,3},{5,4},{6,5},{7,6},{0,7},{9,8},{10,9},{11,1... | collective-permute-start | bytes 3896 | tf_op jit(solution)/shard_map/ppermute | solution.py:24
  103.1 9.5 %collective-permute-start.35 = (f32[18,18,1]{2,1,0:T(8,128)S(1)}, f32[18,18,1]{2,1,0:T(8,128)S(1)}, u32[]{:S(2)}, u32[]{:S(2)}) collective-permute-start(f32[18,18,1]{2,1,0:T(8,128)S(1)} %get-tuple-element.118), channel_id=1, source_target_pairs={{0,1},{1,2},{2,3},{3,4},{4,5},{5,6},{6,7},{7,0},{8,9},{9,10},{10,1... | collective-permute-start | bytes 3896 | tf_op jit(solution)/shard_map/ppermute | solution.py:22
  234.3 22.6 %all-to-all-start = ((f32[256,1,128]{2,1,0:T(1,128)}), f32[256,1,128]{2,1,0:T(1,128)S(1)}, u32[]{:S(2)}, u32[]{:S(2)}) async-start(f32[256,1,128]{2,1,0:T(1,128)} %reshape.93), calls=%async_computation | async-start | bytes 262144 | tf_op jit(solution)/shard_map/all_to_all | solution.py:193
  382.3 11.4 %collective-permute-start.118 = (f32[2,18,18,1]{3,2,1,0:T(8,128)S(1)}, f32[2,18,18,1]{3,2,1,0:T(8,128)S(1)}, u32[]{:S(2)}, u32[]{:S(2)}) collective-permute-start(f32[2,18,18,1]{3,2,1,0:T(8,128)S(1)} %get-tuple-element.87), channel_id=1, source_target_pairs={{0,1},{1,2},{2,3},{3,4},{4,5},{5,6},{6,7},{7,0},{8,9},{9,10},{10,1... | collective-permute-start | bytes 7784 | tf_op jit(solution)/shard_map/ppermute | solution.py:22
  384.6 10.2 %collective-permute-start.119 = (f32[2,18,18,1]{3,2,1,0:T(8,128)S(1)}, f32[2,18,18,1]{3,2,1,0:T(8,128)S(1)}, u32[]{:S(2)}, u32[]{:S(2)}) collective-permute-start(f32[2,18,18,1]{3,2,1,0:T(8,128)S(1)} %get-tuple-element.88), channel_id=1, source_target_pairs={{1,0},{2,1},{3,2},{4,3},{5,4},{6,5},{7,6},{0,7},{9,8},{10,9},{11,1... | collective-permute-start | bytes 7784 | tf_op jit(solution)/shard_map/ppermute | solution.py:24
  405.1 11.5 %collective-permute-start.124 = (f32[2,18,18,1]{3,2,1,0:T(8,128)S(1)}, f32[2,18,18,1]{3,2,1,0:T(8,128)S(1)}, u32[]{:S(2)}, u32[]{:S(2)}) collective-permute-start(f32[2,18,18,1]{3,2,1,0:T(8,128)S(1)} %get-tuple-element.85), channel_id=1, source_target_pairs={{0,1},{1,2},{2,3},{3,4},{4,5},{5,6},{6,7},{7,0},{8,9},{9,10},{10,1... | collective-permute-start | bytes 7784 | tf_op jit(solution)/shard_map/ppermute | solution.py:22
  407.5 11.1 %collective-permute-start.125 = (f32[2,18,18,1]{3,2,1,0:T(8,128)S(1)}, f32[2,18,18,1]{3,2,1,0:T(8,128)S(1)}, u32[]{:S(2)}, u32[]{:S(2)}) collective-permute-start(f32[2,18,18,1]{3,2,1,0:T(8,128)S(1)} %get-tuple-element.86), channel_id=1, source_target_pairs={{1,0},{2,1},{3,2},{4,3},{5,4},{6,5},{7,6},{0,7},{9,8},{10,9},{11,1... | collective-permute-start | bytes 7784 | tf_op jit(solution)/shard_map/ppermute | solution.py:24
  428.4 11.5 %collective-permute-start.130 = (f32[2,18,18,1]{3,2,1,0:T(8,128)S(1)}, f32[2,18,18,1]{3,2,1,0:T(8,128)S(1)}, u32[]{:S(2)}, u32[]{:S(2)}) collective-permute-start(f32[2,18,18,1]{3,2,1,0:T(8,128)S(1)} %get-tuple-element.83), channel_id=1, source_target_pairs={{0,1},{1,2},{2,3},{3,4},{4,5},{5,6},{6,7},{7,0},{8,9},{9,10},{10,1... | collective-permute-start | bytes 7784 | tf_op jit(solution)/shard_map/ppermute | solution.py:22
  429.6 10.5 %collective-permute-start.131 = (f32[2,18,18,1]{3,2,1,0:T(8,128)S(1)}, f32[2,18,18,1]{3,2,1,0:T(8,128)S(1)}, u32[]{:S(2)}, u32[]{:S(2)}) collective-permute-start(f32[2,18,18,1]{3,2,1,0:T(8,128)S(1)} %get-tuple-element.84), channel_id=1, source_target_pairs={{1,0},{2,1},{3,2},{4,3},{5,4},{6,5},{7,6},{0,7},{9,8},{10,9},{11,1... | collective-permute-start | bytes 7784 | tf_op jit(solution)/shard_map/ppermute | solution.py:24
  453.6 8.0 %collective-permute-start.136 = (f32[18,18,1]{2,1,0:T(8,128)S(1)}, f32[18,18,1]{2,1,0:T(8,128)S(1)}, u32[]{:S(2)}, u32[]{:S(2)}) collective-permute-start(f32[18,18,1]{2,1,0:T(8,128)S(1)} %get-tuple-element.115), channel_id=1, source_target_pairs={{1,0},{2,1},{3,2},{4,3},{5,4},{6,5},{7,6},{0,7},{9,8},{10,9},{11,1... | collective-permute-start | bytes 3896 | tf_op jit(solution)/shard_map/ppermute | solution.py:24
  456.9 8.8 %collective-permute-start.137 = (f32[18,18,1]{2,1,0:T(8,128)S(1)}, f32[18,18,1]{2,1,0:T(8,128)S(1)}, u32[]{:S(2)}, u32[]{:S(2)}) collective-permute-start(f32[18,18,1]{2,1,0:T(8,128)S(1)} %get-tuple-element.116), channel_id=1, source_target_pairs={{0,1},{1,2},{2,3},{3,4},{4,5},{5,6},{6,7},{7,0},{8,9},{9,10},{10,1... | collective-permute-start | bytes 3896 | tf_op jit(solution)/shard_map/ppermute | solution.py:22
  (118 other events, 633.3 us)
